TPU v7x, 32 devices: a whole 2x2x4 slice. The times are simulated.
32 devices in a mesh: gene: 8 (over z, x), cell: 4 (over y, core).
Axes of the slice: x: 2, y: 2, z: 4, core: 2. Of those that a mesh axis runs over, the one named last changes fastest.
Arguments:
- gene_tokens: bfloat16 [16, 4096, 768], P('cell', 'gene')
- latents: bfloat16 [64, 768], replicated, may hold values from -6 to 6
- head_temp: float32 [12], replicated, may hold values from 1.5 to 4
- w_key: bfloat16 [768, 768], replicated, may hold values from -0.21875 to 0.21875
- w_value: bfloat16 [768, 768], replicated, may hold values from -0.21875 to 0.21875
- w_out: bfloat16 [768, 768], replicated, may hold values from -0.21875 to 0.21875
- w_set_qkv: bfloat16 [768, 2304], replicated, may hold values from -0.21875 to 0.21875
- w_set_out: bfloat16 [768, 768], replicated, may hold values from -0.21875 to 0.21875
- set_ids: int32 [16], P('cell'), may hold values from 0 to 7, as said below
Outputs:
- latent_states: bfloat16 [16, 64, 768], P('cell', 'gene')
- set_states: bfloat16 [16, 768], P('cell')
Inputs may be any that keep to these rules, and one draw needn't show every extreme that they name: `set_ids`: set s is held by index s mod 4 of cell. At most 2 cells of one device's block belong to sets held by one index, and in every draw one index holds the sets of exactly 2 cells of every device's block.
All inputs are finite; a program needn't handle non-finite values.
Results may differ from a plain program's by a relative error of at most 0.012.
Values may be sent and summed in bfloat16 or wider, within the bound.
A program may use at most 64 MiB of HBM per device.

v0:
```python
import math

import jax
import jax.numpy as jnp
from jax import lax
from jax.sharding import PartitionSpec as P

EPSILON = 1e-06


def head_norm(array, head_count):
    shaped = array.reshape(array.shape[:-1] + (head_count, array.shape[-1] // head_count))
    return shaped * lax.rsqrt(jnp.mean(shaped * shaped, axis=-1, keepdims=True) + EPSILON)


def set_project(inputs, w_set_qkv, head_count):
    model_width = inputs.shape[1]
    head_size = model_width // head_count
    projected = jnp.dot(inputs, w_set_qkv, preferred_element_type=jnp.float32)
    queries = (head_norm(projected[:, :model_width], head_count) / math.sqrt(head_size)).astype(
        jnp.bfloat16
    )
    key_rows = head_norm(projected[:, model_width : 2 * model_width], head_count).astype(
        jnp.bfloat16
    )
    value_rows = (
        projected[:, 2 * model_width :]
        .reshape(inputs.shape[0], head_count, head_size)
        .astype(jnp.bfloat16)
    )
    return (queries, key_rows, value_rows)


def set_attend(queries, key_rows, value_rows, query_ids, key_ids, residual, w_set_out):
    scores = jnp.einsum("qhe,khe->hqk", queries, key_rows, preferred_element_type=jnp.float32)
    matching = query_ids[:, None] == key_ids[None, :]
    weights = jnp.where(matching[None], jnp.exp(scores), 0.0)
    totals = jnp.sum(weights, axis=2)
    numerator = jnp.einsum(
        "hqk,khe->qhe", weights.astype(jnp.bfloat16), value_rows, preferred_element_type=jnp.float32
    )
    attended = (
        (numerator / jnp.transpose(totals)[:, :, None])
        .reshape(queries.shape[0], -1)
        .astype(jnp.bfloat16)
    )
    return (
        residual.astype(jnp.float32)
        + jnp.dot(attended, w_set_out, preferred_element_type=jnp.float32)
    ).astype(jnp.bfloat16)


def on_device(
    gene_tokens, latents, head_temp, w_key, w_value, w_out, w_set_qkv, w_set_out, set_ids
):
    cell_count, gene_count, model_width = gene_tokens.shape
    latent_count = latents.shape[0]
    head_count = head_temp.shape[0]
    head_size = model_width // head_count
    queries = (
        head_norm(latents.astype(jnp.float32), head_count)
        * (head_temp[:, None] / math.sqrt(head_size))
    ).astype(jnp.bfloat16)
    key_rows = head_norm(
        jnp.einsum("cgd,de->cge", gene_tokens, w_key, preferred_element_type=jnp.float32),
        head_count,
    ).astype(jnp.bfloat16)
    value_rows = jnp.einsum(
        "cgd,de->cge", gene_tokens, w_value, preferred_element_type=jnp.float32
    ).astype(jnp.bfloat16)
    value_rows = value_rows.reshape(cell_count, gene_count, head_count, head_size)
    scores = jnp.einsum("lhe,cghe->chlg", queries, key_rows, preferred_element_type=jnp.float32)
    weights = jnp.exp(scores)
    totals = jnp.transpose(jnp.sum(weights, axis=3), (0, 2, 1))
    numerator = jnp.einsum(
        "chlg,cghe->clhe",
        weights.astype(jnp.bfloat16),
        value_rows,
        preferred_element_type=jnp.float32,
    )
    numerator = numerator.reshape(cell_count, latent_count, model_width)
    numerator, totals = (
        lax.psum(numerator.astype(jnp.bfloat16), "gene").astype(jnp.float32),
        lax.psum(totals.astype(jnp.bfloat16), "gene").astype(jnp.float32),
    )
    portion = latent_count // lax.axis_size("gene")
    first_row = lax.axis_index("gene") * portion
    attended = (
        numerator.reshape(cell_count, latent_count, head_count, head_size) / totals[..., None]
    )
    attended = attended.reshape(cell_count, latent_count, model_width).astype(jnp.bfloat16)
    mixed_rows = latents.astype(jnp.float32)[None] + jnp.einsum(
        "cld,de->cle", attended, w_out, preferred_element_type=jnp.float32
    )
    pooled = jnp.mean(mixed_rows, axis=1)
    latent_states = lax.dynamic_slice_in_dim(mixed_rows, first_row, portion, 1).astype(jnp.bfloat16)
    set_input = (
        pooled * lax.rsqrt(jnp.mean(pooled * pooled, axis=1, keepdims=True) + EPSILON)
    ).astype(jnp.bfloat16)
    every_input, every_ids = (
        lax.all_gather(set_input, "cell", axis=0, tiled=True),
        lax.all_gather(set_ids, "cell", axis=0, tiled=True),
    )
    set_queries, set_keys, set_values = set_project(every_input, w_set_qkv, head_count)
    own_queries = lax.dynamic_slice_in_dim(
        set_queries, lax.axis_index("cell") * cell_count, cell_count, 0
    )
    set_states = set_attend(
        own_queries, set_keys, set_values, set_ids, every_ids, set_input, w_set_out
    )
    return (latent_states, set_states)


def solution(mesh):
    in_specs = (P("cell", "gene", None), P(), P(), P(), P(), P(), P(), P(), P("cell"))
    out_specs = (P("cell", "gene", None), P("cell", None))
    return jax.shard_map(
        on_device, mesh=mesh, in_specs=in_specs, out_specs=out_specs, check_vma=False
    )
```

profile of v0, /device:TPU:0, one launch (start us, length us, event | category | flops | bytes accessed | tf_op | source)
XLA Modules:
  0.0 154.6 jit_solution(15478738839907730430)
XLA Ops:
  7.2 2.0 %reshape.103 = f32[64,12,64]{2,1,0:T(8,128)} reshape(bf16[64,768]{1,0:T(8,128)(2,1)} %param.10) | data formatting | bytes 294912 | tf_op jit(solution)/shard_map/reshape | solution.py:12
  9.2 1.3 multiply_reduce_fusion.1
  11.8 5.0 %fusion.8 = f32[4,512,768]{1,2,0:T(8,128)S(1)} fusion(bf16[4,512,768]{2,1,0:T(8,128)(2,1)} %param.9, bf16[768,768]{1,0:T(8,128)(2,1)} %param.12), kind=kOutput, calls=%fused_computation.12 | convolution fusion | flops 2415919104 | bytes 10616832 | tf_op jit(solution)/shard_map/cgd,de->cge/dot_general | solution.py:65
  17.8 2.2 %copy-done.1 = f32[4,512,768]{1,2,0:T(8,128)} copy-done((f32[4,512,768]{1,2,0:T(8,128)}, f32[4,512,768]{1,2,0:T(8,128)S(1)}, u32[]{:S(2)}) %copy-start.1) | copy-done | bytes 6291480
  21.4 4.0 %convolution_convert_fusion = bf16[4,512,768]{2,1,0:T(8,128)(2,1)} fusion(bf16[4,512,768]{2,1,0:T(8,128)(2,1)S(1)} %copy-done.3, bf16[768,768]{1,0:T(8,128)(2,1)S(1)} %copy-done.4), kind=kOutput, calls=%fused_computation.8 | convolution fusion | flops 2417491968 | bytes 7471104 | tf_op jit(solution)/shard_map/cgd,de->cge/dot_general | solution.py:68
  25.3 4.7 %copy.30 = bf16[4,512,768]{1,2,0:T(8,128)(2,1)} copy(bf16[4,512,768]{2,1,0:T(8,128)(2,1)} %convolution_convert_fusion) | data formatting | bytes 6291456 | tf_op jit(solution)/shard_map/convert_element_type | solution.py:70
  30.1 1.2 fusion.15
  31.4 4.8 %bitcast_reduce_fusion = (bf16[4,12,64]{2,0,1:T(4,128)(2,1)}, f32[12,4,512,64]{2,3,1,0:T(8,128)S(1)}) fusion(bf16[64,12,64,1]{2,1,0,3:T(8,128)(2,1)S(1)} %fusion.15, f32[4,512,12,64]{1,3,2,0:T(8,128)} %bitcast.45, f32[4,512,12]{1,2,0:T(8,128)} %add_rsqrt_fusion), kind=kOutput, calls=%fused_computation | convolution fusion | flops 206042112 | bytes 12785664 | tf_op jit(solution)/shard_map/lhe,cghe->chlg/dot_general | solution.py:72
  36.1 1.9 %fusion.4 = bf16[4,12,64,64]{3,2,1,0:T(8,128)(2,1)} fusion(bf16[4,512,12,64]{1,3,2,0:T(8,128)(2,1)S(1)} %bitcast.46, f32[12,4,512,64]{2,3,1,0:T(8,128)S(1)} %get-tuple-element.5), kind=kOutput, calls=%fused_computation.9 | convolution fusion | flops 203096064 | bytes 9830400 | tf_op jit(solution)/shard_map/chlg,cghe->clhe/dot_general | solution.py:75
  38.0 2.1 %copy.35 = bf16[4,64,768]{2,1,0:T(8,128)(2,1)} copy(bf16[4,64,768]{1,2,0:T(8,128)(2,1)} %bitcast.47) | data formatting | bytes 786432 | tf_op jit(solution)/shard_map/convert_element_type | solution.py:83
  40.2 1.6 %convert_element_type.71 = f32[64,768]{1,0:T(8,128)} convert(bf16[64,768]{1,0:T(8,128)(2,1)} %param.10) | non-fusion elementwise | flops 49152 | bytes 294912 | tf_op jit(solution)/shard_map/convert_element_type | solution.py:92
  41.8 38.9 %psum.15 = bf16[4,64,12]{1,0,2:T(4,128)(2,1)S(1)} all-reduce(bf16[4,64,12]{1,0,2:T(4,128)(2,1)} %bitcast.48), channel_id=1, replica_groups=mesh['gene'=8,'cell'=4] {'gene'}, use_global_device_ids=true, to_apply=%region_4.0 | all-reduce | flops 3072 | bytes 12288 | tf_op jit(solution)/shard_map/psum | solution.py:84
  81.5 2.9 %div.60 = f32[4,64,12,64]{3,2,1,0:T(8,128)} broadcast(f32[4,64,12]{2,1,0:T(8,128)} %copy.36), dimensions={0,1,2} | broadcast | bytes 798720 | tf_op jit(solution)/shard_map/div | solution.py:89
  84.4 2.7 %div.61 = f32[4,64,768]{2,1,0:T(8,128)} reshape(f32[4,64,12,64]{3,2,1,0:T(8,128)} %div.60) | data formatting | bytes 1572864 | tf_op jit(solution)/shard_map/div | solution.py:89
  87.1 1.2 dynamic-slice
  89.2 4.9 %all-reduce = s32[16]{0:T(128)S(1)} all-reduce(s32[16]{0:T(128)S(1)} %dynamic-update-slice), channel_id=1, replica_groups=mesh['gene'=8,'cell'=4] {'cell'}, use_global_device_ids=true, to_apply=%add | all-reduce | flops 16 | bytes 128
  94.8 19.7 %all-reduce.3.cloned.1.call-done = bf16[4,64,768]{2,1,0:T(8,128)(2,1)} async-done(((bf16[4,64,768]{2,1,0:T(8,128)(2,1)}), bf16[4,64,768]{2,1,0:T(8,128)(2,1)}) %all-reduce.3.cloned.1.call-update) | async-done | bytes 393232 | tf_op jit(solution)/shard_map/psum | solution.py:83
  114.5 2.9 %fusion.28 = (f32[4,768]{1,0:T(4,128)S(1)}, bf16[4,64,768]{2,1,0:T(8,128)(2,1)}) fusion(bf16[768,768]{1,0:T(8,128)(2,1)} %param.14, f32[4,64,768]{2,1,0:T(8,128)} %div.61, bf16[4,64,768]{2,1,0:T(8,128)(2,1)} %all-reduce.3.cloned.1.call-done, f32[64,768]{1,0:T(8,128)} %convert_element_type.71), kind=kOutput, calls=%fused_computation.55 | convolution fusion | flops 303166464 | bytes 2961408 | tf_op jit(solution)/shard_map/cld,de->cle/dot_general | solution.py:92
  117.5 5.6 %all-gather = bf16[4,4,768]{2,1,0:T(4,128)(2,1)} all-gather(bf16[1,4,768]{2,1,0:T(4,128)(2,1)S(1)} %fusion.26), channel_id=1, replica_groups=mesh['gene'=8,'cell'=4] {'cell'}, dimensions={0}, use_global_device_ids=true | all-gather | bytes 30720 | tf_op jit(solution)/shard_map/all_gather | solution.py:101
  123.2 1.4 reshape.110
  124.5 1.3 fusion.30
  127.1 1.5 reshape.105
  129.7 1.6 %multiply_convert_fusion.2 = bf16[16,12,64]{2,1,0:T(8,128)(2,1)} fusion(f32[16,12,64]{2,1,0:T(8,128)} %reshape.105, f32[16,12]{1,0:T(8,128)S(1)} %add_rsqrt_fusion.2), kind=kLoop, calls=%fused_computation.27 | loop fusion | flops 24576 | bytes 74496 | tf_op jit(solution)/shard_map/convert_element_type | solution.py:23
  131.3 1.5 reshape.104
  133.8 1.4 constant_dynamic-slice_fusion
  135.8 1.4 copy.37
  137.2 1.4 constant_dynamic-slice_fusion.1
  138.6 1.5 convert_element_type.87
  140.0 1.2 fusion.29
  142.8 1.4 convert_element_type.92
  144.2 2.2 %fusion.14 = bf16[4,768]{1,0:T(4,128)(2,1)} fusion(bf16[4,768]{1,0:T(4,128)(2,1)} %convert_element_type.92, bf16[768,768]{1,0:T(8,128)(2,1)} %param.16, f32[4,768]{1,0:T(4,128)S(1)} %get-tuple-element.6, f32[4]{0:T(128)S(1)} %rsqrt_multiply_fusion), kind=kOutput, calls=%fused_computation.21 | convolution fusion | flops 4733952 | bytes 1204240 | tf_op jit(solution)/shard_map/dot_general | solution.py:49
  146.3 1.4 dynamic-slice_convert_fusion
  (32 shorter events, 10.9 us)
Async XLA Ops:
  7.2 117.4 %copy-start = (bf16[768,2304]{1,0:T(8,128)(2,1)S(1)}, bf16[768,2304]{1,0:T(8,128)(2,1)}, u32[]{:S(2)}) copy-start(bf16[768,2304]{1,0:T(8,128)(2,1)} %param.15) | copy-start | bytes 10616836
  7.2 107.3 %all-reduce.3.cloned.1.call-start = ((), (), s32[]{:S(2)}) async-start(), calls=%async_computation | async-start | bytes 786432 | tf_op jit(solution)/shard_map/psum | solution.py:83
  16.8 3.2 %copy-start.1 = (f32[4,512,768]{1,2,0:T(8,128)}, f32[4,512,768]{1,2,0:T(8,128)S(1)}, u32[]{:S(2)}) copy-start(f32[4,512,768]{1,2,0:T(8,128)S(1)} %fusion.8) | copy-start | bytes 18874372
  16.8 4.2 %copy-start.3 = (bf16[4,512,768]{2,1,0:T(8,128)(2,1)S(1)}, bf16[4,512,768]{2,1,0:T(8,128)(2,1)}, u32[]{:S(2)}) copy-start(bf16[4,512,768]{2,1,0:T(8,128)(2,1)} %param.9) | copy-start | bytes 9437188
  16.8 4.5 %copy-start.4 = (bf16[768,768]{1,0:T(8,128)(2,1)S(1)}, bf16[768,768]{1,0:T(8,128)(2,1)}, u32[]{:S(2)}) copy-start(bf16[768,768]{1,0:T(8,128)(2,1)} %param.13) | copy-start | bytes 3538948
  31.3 4.8 %copy-start.2 = (bf16[4,512,768]{1,2,0:T(8,128)(2,1)S(1)}, bf16[4,512,768]{1,2,0:T(8,128)(2,1)}, u32[]{:S(2)}) copy-start(bf16[4,512,768]{1,2,0:T(8,128)(2,1)} %copy.30) | copy-start | bytes 9437188
  40.2 48.8 %copy-start.5 = (s32[4]{0:T(128)S(1)}, s32[4]{0:T(128)}, u32[]{:S(2)}) copy-start(s32[4]{0:T(128)} %param.17) | copy-start | bytes 52
Sparse Core Ops, SparseCore 0:
  40.3 74.0 all-reduce.2
where the time goes:
time: 156 us; the launch traced here: 155 us
  blocking collectives  49.5 us (32%)
  local copies, waits for them, and re-layouts  34.3 us (22%)
  matrix products  24.2 us (16%)
  waiting for transfers between devices  19.7 us (13%)
  between operations  14.8 us (9%)
  other arithmetic  12.1 us (8%)
    psum x1, blocking collectives, on_device(): lax.psum(totals.astype(jnp.bfloat16), 'gene').astype(jnp.float32)  38.9 us
    psum x1, waiting for transfers between devices, on_device(): lax.psum(numerator.astype(jnp.bfloat16), 'gene').astype(jnp.float32)  19.7 us
    unnamed x16, local copies, waits for them, and re-layouts  5.73 us
    all_gather x1, blocking collectives, on_device(): lax.all_gather(set_input, 'cell', axis=0, tiled=True)  5.63 us
    div x2, local copies, waits for them, and re-layouts, on_device(): numerator.reshape(cell_count, latent_count, head_count, head_size)  5.58 us
    reshape x3, local copies, waits for them, and re-layouts, head_norm(): array.reshape(array.shape[:-1] + (head_count, array.shape[-1] // head_cou...  5.07 us
    dot_general x1, matrix products, on_device(): jnp.einsum('cgd,de->cge', gene_tokens, w_key, preferred_element_type=jnp....  5.02 us
    unnamed x1, blocking collectives  4.93 us
  transfers between devices with their start and end apart: 1, of which 1 were waited for; matrix products, arithmetic and copies ran while one was open for 6% of the time, Pallas kernels for 0%

commit v1 on v0

v1 whole, which is shorter than its diff:
```python
import functools
import math

import jax
import jax.numpy as jnp
from jax import lax
from jax.experimental import pallas as pl
from jax.experimental.pallas import tpu as pltpu
from jax.sharding import PartitionSpec as P

EPSILON = 1e-06
MESH = pl.DeviceIdType.MESH
F32, BF16 = jnp.float32, jnp.bfloat16
HEAD = 64
LANES = 128
GROUP = 256
ROWS = 8


def iota(shape, dim):
    return lax.broadcasted_iota(jnp.int32, shape, dim)


def dot(a, b):
    return jnp.dot(a, b, preferred_element_type=F32)


def dot_nt(a, b):
    return lax.dot_general(a, b, (((1,), (1,)), ((), ())), preferred_element_type=F32)


def dot_split(a, b):
    high = a.astype(BF16)
    low = (a - high.astype(F32)).astype(BF16)
    return dot(high, b) + dot(low, b)


def kernel(
    n,
    m,
    tok_hbm,
    lat_hbm,
    temp_ref,
    wk_hbm,
    wv_hbm,
    wo_hbm,
    wqkv_hbm,
    wso_hbm,
    ids_ref,
    lat_out,
    set_out,
    tok,
    lat,
    wk,
    wv,
    wo,
    wqkv,
    wso,
    qb,
    send,
    recv,
    acc,
    psum,
    psend,
    precv,
    ssend,
    srecv,
    in_sem,
    tok_sem,
    send_sem,
    recv_sem,
    late_sem,
):
    cells, genes, width = tok.shape
    latents = lat.shape[0]
    portion = latents // n
    heads = width // HEAD
    groups = width // GROUP
    per_group = GROUP // HEAD
    half = width // 2
    gene = lax.axis_index("gene")
    cell = lax.axis_index("cell")

    barrier = pltpu.get_barrier_semaphore()
    for o in range(1, n):
        pl.semaphore_signal(
            barrier, inc=1, device_id=(lax.rem(gene + o, n), cell), device_id_type=MESH
        )
    for o in range(1, m):
        pl.semaphore_signal(
            barrier, inc=1, device_id=(gene, lax.rem(cell + o, m)), device_id_type=MESH
        )

    lat_in = pltpu.make_async_copy(lat_hbm, lat, in_sem.at[0])
    wk_in = pltpu.make_async_copy(wk_hbm, wk, in_sem.at[1])
    wv_in = pltpu.make_async_copy(wv_hbm, wv, in_sem.at[2])
    wo_in = pltpu.make_async_copy(wo_hbm, wo, in_sem.at[3])
    wqkv_in = pltpu.make_async_copy(wqkv_hbm, wqkv, in_sem.at[4])
    wso_in = pltpu.make_async_copy(wso_hbm, wso, in_sem.at[5])

    def tok_in(c):
        return pltpu.make_async_copy(tok_hbm.at[c], tok.at[c], tok_sem.at[c])

    lat_in.start()
    wk_in.start()
    tok_in(0).start()
    wv_in.start()
    for c in range(1, cells):
        tok_in(c).start()
    wo_in.start()
    wqkv_in.start()
    wso_in.start()

    same_head = (iota((GROUP, GROUP), 0) >> 6) == (iota((GROUP, GROUP), 1) >> 6)
    mean_head = jnp.where(same_head, 1.0 / HEAD, 0.0).astype(BF16)
    col_head = iota((latents, GROUP), 1) >> 6
    lane = iota((latents, LANES), 1)

    def head_scale(x):
        return lax.rsqrt(dot((x * x).astype(BF16), mean_head) + EPSILON)

    lat_in.wait()
    for i in range(groups):
        block = lat[:, i * GROUP : (i + 1) * GROUP].astype(F32)
        mean_square = dot_split(block * block, mean_head)
        temp = jnp.zeros((latents, GROUP), F32)
        for h in range(per_group):
            temp = jnp.where(
                col_head == h, temp_ref[i * per_group + h] / math.sqrt(HEAD), temp
            )
        query = block * lax.rsqrt(mean_square + EPSILON) * temp
        stacked = jnp.concatenate([query] * per_group, axis=0)
        qb[i] = jnp.where(same_head, stacked, 0.0).astype(BF16)

    wk_in.wait()
    wv_in.wait()
    pl.semaphore_wait(barrier, n - 1 + m - 1)

    def one_cell(c, carry):
        tok_in(c).wait()
        tokens = tok[c]
        totals = jnp.zeros((latents, LANES), F32)
        for i in range(groups):
            cols = slice(i * GROUP, (i + 1) * GROUP)
            key = dot(tokens, wk[:, cols])
            key = (key * head_scale(key)).astype(BF16)
            weights = jnp.exp(dot_nt(qb[i], key))
            value = dot(tokens, wv[:, cols]).astype(BF16)
            mixed = dot(weights.astype(BF16), value)
            total = jnp.sum(weights, axis=1, keepdims=True)
            numerator = mixed[:latents]
            for h in range(per_group):
                rows = slice(h * latents, (h + 1) * latents)
                numerator = jnp.where(col_head == h, mixed[rows], numerator)
                totals = jnp.where(lane == i * per_group + h, total[rows], totals)
            for j in range(n):
                send[c, j, :, cols] = numerator[j * portion : (j + 1) * portion].astype(BF16)
        for j in range(n):
            send[c, j, :, width:] = totals[j * portion : (j + 1) * portion].astype(BF16)
        for o in range(1, n):
            peer = lax.rem(gene + o, n)
            pltpu.make_async_remote_copy(
                src_ref=send.at[c, peer],
                dst_ref=recv.at[c, o],
                send_sem=send_sem.at[c],
                recv_sem=recv_sem.at[c],
                device_id=(peer, cell),
                device_id_type=MESH,
            ).start()
        return carry

    lax.fori_loop(0, cells, one_cell, 0)

    select = iota((cells * portion, latents), 0)
    select = lax.rem(select, portion) + gene * portion == iota((cells * portion, latents), 1)
    own_latents = dot(select.astype(F32).astype(BF16), lat[...])
    mean_latents = jnp.sum(lat[...].astype(F32), axis=0, keepdims=True) * (1.0 / latents)
    expand = iota((LANES, width), 0) == (iota((LANES, width), 1) >> 6)
    expand = expand.astype(F32).astype(BF16)
    one_hot = jnp.zeros((ROWS, LANES), F32)
    row8, lane8 = iota((ROWS, LANES), 0), iota((ROWS, LANES), 1)
    for c in range(cells):
        one_hot = jnp.where((row8 == c) & (lane8 == ids_ref[c]), 1.0, one_hot)

    for c in range(cells):
        arrived = pltpu.make_async_remote_copy(
            src_ref=send.at[c, pl.ds(0, n - 1)],
            dst_ref=recv.at[c, pl.ds(1, n - 1)],
            send_sem=send_sem.at[c],
            recv_sem=recv_sem.at[c],
            device_id=(gene, cell),
            device_id_type=MESH,
        )
        arrived.wait_recv()
        total = send[c, gene].astype(F32)
        for o in range(1, n):
            total = total + recv[c, o].astype(F32)
        acc[c * portion : (c + 1) * portion, :] = total
        arrived.wait_send()
    totals = acc[:, width:]
    is_head = iota(totals.shape, 1) < heads
    inverse = jnp.where(is_head, 1.0 / jnp.where(is_head, totals, 1.0), 0.0)
    attended = (acc[:, :width] * dot_split(inverse, expand)).astype(BF16)
    wide = attended.astype(F32)
    for c in range(cells):
        row = jnp.sum(wide[c * portion : (c + 1) * portion], axis=0, keepdims=True)
        psum[c : c + 1, :] = row[:, :half]
        psum[cells + c : cells + c + 1, :] = row[:, half:]
    psend[...] = psum[...].astype(BF16)
    for o in range(1, n):
        pltpu.make_async_remote_copy(
            src_ref=psend,
            dst_ref=precv.at[o],
            send_sem=late_sem.at[0],
            recv_sem=late_sem.at[1],
            device_id=(lax.rem(gene + o, n), cell),
            device_id_type=MESH,
        ).start()

    wo_in.wait()
    mixed_rows = own_latents + dot(attended, wo[...])
    for c in range(cells):
        lat_out[c] = mixed_rows[c * portion : (c + 1) * portion].astype(BF16)

    wqkv_in.wait()
    wso_in.wait()
    arrived = pltpu.make_async_remote_copy(
        src_ref=precv.at[pl.ds(1, n - 1)],
        dst_ref=precv.at[pl.ds(1, n - 1)],
        send_sem=late_sem.at[0],
        recv_sem=late_sem.at[1],
        device_id=(gene, cell),
        device_id_type=MESH,
    )
    arrived.wait_recv()
    summed = psend[...].astype(F32)
    for o in range(1, n):
        summed = summed + precv[o].astype(F32)
    arrived.wait_send()
    summed = jnp.concatenate([summed, pltpu.roll(summed, ROWS - cells, 0)], axis=1)
    pooled = mean_latents + dot_split(summed * (1.0 / latents), wo[...])
    scale = lax.rsqrt(jnp.mean(pooled * pooled, axis=1, keepdims=True) + EPSILON)
    own_input = (pooled * scale).astype(BF16)
    ssend[:, :width] = own_input.astype(F32)
    ssend[:, width:] = one_hot
    for o in range(1, m):
        pltpu.make_async_remote_copy(
            src_ref=ssend,
            dst_ref=srecv.at[o],
            send_sem=late_sem.at[2],
            recv_sem=late_sem.at[3],
            device_id=(gene, lax.rem(cell + o, m)),
            device_id_type=MESH,
        ).start()

    def head_rows(x):
        parts = []
        for i in range(groups):
            part = x[:, i * GROUP : (i + 1) * GROUP]
            parts.append(part * head_scale(part))
        return jnp.concatenate(parts, axis=1)

    stack = (heads * ROWS, width)
    own_head = (iota(stack, 0) >> 3) == (iota(stack, 1) >> 6)
    queries = head_rows(dot(own_input, wqkv[:, :width])) * (1.0 / math.sqrt(HEAD))
    queries = jnp.concatenate([queries] * heads, axis=0)
    queries = jnp.where(own_head, queries, 0.0).astype(BF16)
    query_sets = jnp.concatenate([one_hot] * heads, axis=0).astype(BF16)

    arrived = pltpu.make_async_remote_copy(
        src_ref=srecv.at[pl.ds(1, m - 1)],
        dst_ref=srecv.at[pl.ds(1, m - 1)],
        send_sem=late_sem.at[2],
        recv_sem=late_sem.at[3],
        device_id=(gene, cell),
        device_id_type=MESH,
    )
    arrived.wait_recv()
    every = jnp.concatenate([ssend[...]] + [srecv[o] for o in range(1, m)], axis=0).astype(BF16)
    arrived.wait_send()
    every_input, key_sets = every[:, :width], every[:, width:]
    keys_values = dot(every_input, wqkv[:, width:])
    keys = head_rows(keys_values[:, :width]).astype(BF16)
    values = keys_values[:, width:].astype(BF16)
    matching = dot_nt(query_sets, key_sets) > 0.5
    weights = jnp.where(matching, jnp.exp(dot_nt(queries, keys)), 0.0)
    total = jnp.sum(weights, axis=1, keepdims=True)
    total = jnp.where(total > 0.0, total, 1.0)
    mixed = jnp.where(own_head, dot(weights.astype(BF16), values) / total, 0.0)
    set_attended = mixed[:ROWS]
    for h in range(1, heads):
        set_attended = set_attended + mixed[h * ROWS : (h + 1) * ROWS]
    states = own_input.astype(F32) + dot(set_attended.astype(BF16), wso[...])
    set_out[...] = states[:cells].astype(BF16)


def on_device(
    n, m, gene_tokens, latents, head_temp, w_key, w_value, w_out, w_set_qkv, w_set_out, set_ids
):
    cells, genes, width = gene_tokens.shape
    rows = latents.shape[0]
    portion = rows // n
    hbm = pl.BlockSpec(memory_space=pltpu.HBM)
    smem = pl.BlockSpec(memory_space=pltpu.SMEM)
    vmem = pl.BlockSpec(memory_space=pltpu.VMEM)
    wide = width + LANES
    return tuple(
        pl.pallas_call(
            functools.partial(kernel, n, m),
            out_shape=(
                jax.ShapeDtypeStruct((cells, portion, width), BF16),
                jax.ShapeDtypeStruct((cells, width), BF16),
            ),
            in_specs=[hbm, hbm, smem, hbm, hbm, hbm, hbm, hbm, smem],
            out_specs=(vmem, vmem),
            scratch_shapes=[
                pltpu.VMEM(gene_tokens.shape, BF16),
                pltpu.VMEM(latents.shape, BF16),
                pltpu.VMEM(w_key.shape, BF16),
                pltpu.VMEM(w_value.shape, BF16),
                pltpu.VMEM(w_out.shape, BF16),
                pltpu.VMEM(w_set_qkv.shape, BF16),
                pltpu.VMEM(w_set_out.shape, BF16),
                pltpu.VMEM((width // GROUP, GROUP, GROUP), BF16),
                pltpu.VMEM((cells, n, portion, wide), BF16),
                pltpu.VMEM((cells, n, portion, wide), BF16),
                pltpu.VMEM((cells * portion, wide), F32),
                pltpu.VMEM((ROWS, width // 2), F32),
                pltpu.VMEM((ROWS, width // 2), BF16),
                pltpu.VMEM((n, ROWS, width // 2), BF16),
                pltpu.VMEM((ROWS, wide), F32),
                pltpu.VMEM((m, ROWS, wide), F32),
                pltpu.SemaphoreType.DMA((6,)),
                pltpu.SemaphoreType.DMA((cells,)),
                pltpu.SemaphoreType.DMA((cells,)),
                pltpu.SemaphoreType.DMA((cells,)),
                pltpu.SemaphoreType.DMA((4,)),
            ],
            compiler_params=pltpu.CompilerParams(
                collective_id=0, has_side_effects=True, vmem_limit_bytes=50 * 1024 * 1024
            ),
            name="latent_cross_attention",
        )(gene_tokens, latents, head_temp, w_key, w_value, w_out, w_set_qkv, w_set_out, set_ids)
    )


def solution(mesh):
    n, m = mesh.shape["gene"], mesh.shape["cell"]
    in_specs = (P("cell", "gene", None), P(), P(), P(), P(), P(), P(), P(), P("cell"))
    out_specs = (P("cell", "gene", None), P("cell", None))
    return jax.shard_map(
        functools.partial(on_device, n, m),
        mesh=mesh,
        in_specs=in_specs,
        out_specs=out_specs,
        check_vma=False,
    )
```

time: 156 us -> 43.5 us (0.28)
  blocking collectives: 49.5 us -> 0 us
  Pallas kernels: 0 us -> 35.4 us
  local copies, waits for them, and re-layouts: 34.3 us -> 7.22 us
  matrix products: 24.2 us -> 0 us
  waiting for transfers between devices: 19.7 us -> 0 us
  between operations: 14.8 us -> 0.66 us
  other arithmetic: 12.1 us -> 0 us
    psum x1 -> x0, blocking collectives: 38.9 us -> none  [on_device(): lax.psum(totals.astype(jnp.bfloat16), 'gene').astype(jnp.float32)]
    pallas_call x0 -> x1, Pallas kernels: none -> 35.4 us  [on_device(): pl.pallas_call(functools.partial(kernel, n, m), out_shape=(jax.ShapeDtype...]
    dot_general x9 -> x0, matrix products: 24.2 us -> none  [the longest x1 5.02 us: on_device(): jnp.einsum('cgd,de->cge', gene_tokens, w_key, preferred_element_type=jnp....]
    psum x1 -> x0, waiting for transfers between devices: 19.7 us -> none  [on_device(): lax.psum(numerator.astype(jnp.bfloat16), 'gene').astype(jnp.float32)]
    convert_element_type x7 -> x0, local copies, waits for them, and re-layouts: 12.5 us -> none  [the longest x1 4.74 us: on_device(): value_rows = jnp.einsum('cgd,de->cge', gene_tokens, w_value, preferred_el...]
    all_gather x1 -> x0, blocking collectives: 5.63 us -> none  [on_device(): lax.all_gather(set_input, 'cell', axis=0, tiled=True)]
    div x2 -> x0, local copies, waits for them, and re-layouts: 5.58 us -> none  [on_device(): numerator.reshape(cell_count, latent_count, head_count, head_size)]
    reshape x3 -> x0, local copies, waits for them, and re-layouts: 5.07 us -> none  [head_norm(): array.reshape(array.shape[:-1] + (head_count, array.shape[-1] // head_cou...]
  transfers between devices with their start and end apart: 1 -> 0, of which waited for: 1 -> 0; matrix products, arithmetic and copies ran while one was open for 6% -> 0% of each run, Pallas kernels for 0% -> 0%
where the time goes in v1:
time: 43.5 us; the launch traced here: 43.3 us
  Pallas kernels  35.4 us (81%)
  local copies, waits for them, and re-layouts  7.22 us (17%)
  between operations  0.66 us (2%)
    pallas_call x1, Pallas kernels, on_device(): pl.pallas_call(functools.partial(kernel, n, m), out_shape=(jax.ShapeDtype...  35.4 us
    unnamed x14, local copies, waits for them, and re-layouts  7.22 us

profile of v1, /device:TPU:0, one launch (start us, length us, event | category | flops | bytes accessed | tf_op | source)
XLA Modules:
  0.0 43.3 jit_solution(16966290979838771530)
XLA Ops:
  0.6 0.0 copy-start
  0.6 1.3 %copy-done = bf16[768,768]{1,0:T(8,128)(2,1)S(1)} copy-done((bf16[768,768]{1,0:T(8,128)(2,1)S(1)}, bf16[768,768]{1,0:T(8,128)(2,1)}, u32[]{:S(2)}) %copy-start) | copy-done | bytes 1179672
  1.9 0.0 copy-start.1
  1.9 1.3 %copy-done.1 = bf16[768,768]{1,0:T(8,128)(2,1)S(1)} copy-done((bf16[768,768]{1,0:T(8,128)(2,1)S(1)}, bf16[768,768]{1,0:T(8,128)(2,1)}, u32[]{:S(2)}) %copy-start.1) | copy-done | bytes 1179672
  3.2 0.0 copy-start.2
  3.2 1.3 %copy-done.2 = bf16[768,768]{1,0:T(8,128)(2,1)S(1)} copy-done((bf16[768,768]{1,0:T(8,128)(2,1)S(1)}, bf16[768,768]{1,0:T(8,128)(2,1)}, u32[]{:S(2)}) %copy-start.2) | copy-done | bytes 1179672
  4.4 0.0 copy-start.3
  4.4 0.9 %copy-done.3 = bf16[64,768]{1,0:T(8,128)(2,1)S(1)} copy-done((bf16[64,768]{1,0:T(8,128)(2,1)S(1)}, bf16[64,768]{1,0:T(8,128)(2,1)}, u32[]{:S(2)}) %copy-start.3) | copy-done | bytes 98328
  5.3 0.0 copy-start.4
  5.3 0.7 %copy-done.4 = f32[12]{0:T(128)S(1)} copy-done((f32[12]{0:T(128)S(1)}, f32[12]{0:T(128)}, u32[]{:S(2)}) %copy-start.4) | copy-done | bytes 72
  6.0 0.0 copy-start.5
  6.0 0.7 %copy-done.5 = s32[4]{0:T(128)S(1)} copy-done((s32[4]{0:T(128)S(1)}, s32[4]{0:T(128)}, u32[]{:S(2)}) %copy-start.5) | copy-done | bytes 40
  6.7 35.4 %latent_cross_attention.1 = (bf16[4,8,768]{2,1,0:T(8,128)(2,1)S(1)}, bf16[4,768]{1,0:T(4,128)(2,1)S(1)}) custom-call(bf16[4,512,768]{2,1,0:T(8,128)(2,1)} %tok_hbm.1, bf16[64,768]{1,0:T(8,128)(2,1)S(1)} %copy-done.3, f32[12]{0:T(128)S(1)} %copy-done.4, bf16[768,768]{1,0:T(8,128)(2,1)S(1)} %copy-done, bf16[768,768]{1,0:T(8,128)(2,1)S(1)} %copy-done.1, ...), custom_call_target="tpu_custom_call" | custom-call | tf_op jit(solution)/shard_map/latent_cross_attention/pallas_call | solution.py:308
  42.1 0.6 %copy.13 = bf16[4,8,768]{2,1,0:T(8,128)(2,1)} copy(bf16[4,8,768]{2,1,0:T(8,128)(2,1)S(1)} %get-tuple-element.4) | data formatting | bytes 98304
  42.7 0.6 %copy.14 = bf16[4,768]{1,0:T(4,128)(2,1)} copy(bf16[4,768]{1,0:T(4,128)(2,1)S(1)} %get-tuple-element.5) | data formatting | bytes 12288
Async XLA Ops:
  0.6 1.3 %copy-start = (bf16[768,768]{1,0:T(8,128)(2,1)S(1)}, bf16[768,768]{1,0:T(8,128)(2,1)}, u32[]{:S(2)}) copy-start(bf16[768,768]{1,0:T(8,128)(2,1)} %wk_hbm.1) | copy-start | bytes 3538948
  1.9 1.3 %copy-start.1 = (bf16[768,768]{1,0:T(8,128)(2,1)S(1)}, bf16[768,768]{1,0:T(8,128)(2,1)}, u32[]{:S(2)}) copy-start(bf16[768,768]{1,0:T(8,128)(2,1)} %wv_hbm.1) | copy-start | bytes 3538948
  3.2 1.3 %copy-start.2 = (bf16[768,768]{1,0:T(8,128)(2,1)S(1)}, bf16[768,768]{1,0:T(8,128)(2,1)}, u32[]{:S(2)}) copy-start(bf16[768,768]{1,0:T(8,128)(2,1)} %wo_hbm.1) | copy-start | bytes 3538948
  4.4 0.9 %copy-start.3 = (bf16[64,768]{1,0:T(8,128)(2,1)S(1)}, bf16[64,768]{1,0:T(8,128)(2,1)}, u32[]{:S(2)}) copy-start(bf16[64,768]{1,0:T(8,128)(2,1)} %lat_hbm.1) | copy-start | bytes 294916
  5.3 0.7 %copy-start.4 = (f32[12]{0:T(128)S(1)}, f32[12]{0:T(128)}, u32[]{:S(2)}) copy-start(f32[12]{0:T(128)} %temp_ref.1) | copy-start | bytes 148
  6.0 0.7 %copy-start.5 = (s32[4]{0:T(128)S(1)}, s32[4]{0:T(128)}, u32[]{:S(2)}) copy-start(s32[4]{0:T(128)} %ids_ref.1) | copy-start | bytes 52

commit v2 on v1

--- a/solution.py
+++ b/solution.py
@@ -14,6 +14,7 @@
 HEAD = 64
 LANES = 128
 GROUP = 256
+VMEM_BYTES = 63 * 1024 * 1024
 ROWS = 8
 
 
@@ -40,13 +41,13 @@
     m,
     tok_hbm,
     lat_hbm,
-    temp_ref,
+    temp_hbm,
     wk_hbm,
     wv_hbm,
     wo_hbm,
     wqkv_hbm,
     wso_hbm,
-    ids_ref,
+    ids_hbm,
     lat_out,
     set_out,
     tok,
@@ -65,6 +66,8 @@
     precv,
     ssend,
     srecv,
+    temp_ref,
+    ids_ref,
     in_sem,
     tok_sem,
     send_sem,
@@ -97,11 +100,15 @@
     wo_in = pltpu.make_async_copy(wo_hbm, wo, in_sem.at[3])
     wqkv_in = pltpu.make_async_copy(wqkv_hbm, wqkv, in_sem.at[4])
     wso_in = pltpu.make_async_copy(wso_hbm, wso, in_sem.at[5])
+    temp_in = pltpu.make_async_copy(temp_hbm, temp_ref, in_sem.at[6])
+    ids_in = pltpu.make_async_copy(ids_hbm, ids_ref, in_sem.at[7])
 
     def tok_in(c):
         return pltpu.make_async_copy(tok_hbm.at[c], tok.at[c], tok_sem.at[c])
 
     lat_in.start()
+    temp_in.start()
+    ids_in.start()
     wk_in.start()
     tok_in(0).start()
     wv_in.start()
@@ -120,6 +127,8 @@
         return lax.rsqrt(dot((x * x).astype(BF16), mean_head) + EPSILON)
 
     lat_in.wait()
+    temp_in.wait()
+    ids_in.wait()
     for i in range(groups):
         block = lat[:, i * GROUP : (i + 1) * GROUP].astype(F32)
         mean_square = dot_split(block * block, mean_head)
@@ -301,7 +310,6 @@
     rows = latents.shape[0]
     portion = rows // n
     hbm = pl.BlockSpec(memory_space=pltpu.HBM)
-    smem = pl.BlockSpec(memory_space=pltpu.SMEM)
     vmem = pl.BlockSpec(memory_space=pltpu.VMEM)
     wide = width + LANES
     return tuple(
@@ -311,7 +319,7 @@
                 jax.ShapeDtypeStruct((cells, portion, width), BF16),
                 jax.ShapeDtypeStruct((cells, width), BF16),
             ),
-            in_specs=[hbm, hbm, smem, hbm, hbm, hbm, hbm, hbm, smem],
+            in_specs=[hbm] * 9,
             out_specs=(vmem, vmem),
             scratch_shapes=[
                 pltpu.VMEM(gene_tokens.shape, BF16),
@@ -330,14 +338,16 @@
                 pltpu.VMEM((n, ROWS, width // 2), BF16),
                 pltpu.VMEM((ROWS, wide), F32),
                 pltpu.VMEM((m, ROWS, wide), F32),
-                pltpu.SemaphoreType.DMA((6,)),
+                pltpu.SMEM(head_temp.shape, F32),
+                pltpu.SMEM(set_ids.shape, jnp.int32),
+                pltpu.SemaphoreType.DMA((8,)),
                 pltpu.SemaphoreType.DMA((cells,)),
                 pltpu.SemaphoreType.DMA((cells,)),
                 pltpu.SemaphoreType.DMA((cells,)),
                 pltpu.SemaphoreType.DMA((4,)),
             ],
             compiler_params=pltpu.CompilerParams(
-                collective_id=0, has_side_effects=True, vmem_limit_bytes=50 * 1024 * 1024
+                collective_id=0, has_side_effects=True, vmem_limit_bytes=VMEM_BYTES
             ),
             name="latent_cross_attention",
         )(gene_tokens, latents, head_temp, w_key, w_value, w_out, w_set_qkv, w_set_out, set_ids)

time: 43.5 us -> 39 us (0.90)
  local copies, waits for them, and re-layouts: 7.22 us -> 2.71 us
    unnamed x14 -> x2, local copies, waits for them, and re-layouts: 7.22 us -> 2.71 us
where the time goes in v2:
time: 39 us; the launch traced here: 38.8 us
  Pallas kernels  35.5 us (91%)
  local copies, waits for them, and re-layouts  2.71 us (7%)
  between operations  0.64 us (2%)
    pallas_call x1, Pallas kernels, on_device(): pl.pallas_call(functools.partial(kernel, n, m), out_shape=(jax.ShapeDtype...  35.5 us
    unnamed x2, local copies, waits for them, and re-layouts  2.71 us

profile of v2, /device:TPU:0, one launch (start us, length us, event | category | flops | bytes accessed | tf_op | source)
XLA Modules:
  0.0 38.8 jit_solution(661971597427771650)
XLA Ops:
  0.6 35.5 %latent_cross_attention.1 = (bf16[4,8,768]{2,1,0:T(8,128)(2,1)}, bf16[4,768]{1,0:T(4,128)(2,1)}) custom-call(bf16[4,512,768]{2,1,0:T(8,128)(2,1)} %tok_hbm.1, bf16[64,768]{1,0:T(8,128)(2,1)} %lat_hbm.1, f32[12]{0:T(128)} %temp_hbm.1, bf16[768,768]{1,0:T(8,128)(2,1)} %wk_hbm.1, bf16[768,768]{1,0:T(8,128)(2,1)} %wv_hbm.1, bf16[768,768]{1,0:T(8,128)(2,1)} %wo_hbm.1, ...), custom_call_target="tpu_custom_call" | custom-call | tf_op jit(solution)/shard_map/latent_cross_attention/pallas_call | solution.py:316
  36.1 1.4 %copy.13 = bf16[4,8,768]{2,1,0:T(8,128)(2,1)} copy(bf16[4,8,768]{2,1,0:T(8,128)(2,1)} %get-tuple-element.4) | data formatting | bytes 98304
  37.5 1.3 %copy.14 = bf16[4,768]{1,0:T(4,128)(2,1)} copy(bf16[4,768]{1,0:T(4,128)(2,1)} %get-tuple-element.5) | data formatting | bytes 12288

commit v3 on v2

--- a/solution.py
+++ b/solution.py
@@ -33,7 +33,8 @@
 def dot_split(a, b):
     high = a.astype(BF16)
     low = (a - high.astype(F32)).astype(BF16)
-    return dot(high, b) + dot(low, b)
+    both = dot(jnp.concatenate([high, low], axis=0), b)
+    return both[: a.shape[0]] + both[a.shape[0] :]
 
 
 def kernel(
@@ -66,6 +67,11 @@
     precv,
     ssend,
     srecv,
+    tsend,
+    trecv,
+    hsend,
+    hrecv,
+    inv,
     temp_ref,
     ids_ref,
     in_sem,
@@ -123,6 +129,9 @@
     col_head = iota((latents, GROUP), 1) >> 6
     lane = iota((latents, LANES), 1)
 
+    def side_by_side(x):
+        return jnp.concatenate([x, pltpu.roll(x, ROWS - cells, 0)], axis=1)
+
     def head_scale(x):
         return lax.rsqrt(dot((x * x).astype(BF16), mean_head) + EPSILON)
 
@@ -143,29 +152,45 @@
 
     wk_in.wait()
     wv_in.wait()
+    one_hot = jnp.zeros((ROWS, LANES), F32)
+    row8, lane8 = iota((ROWS, LANES), 0), iota((ROWS, LANES), 1)
+    for c in range(cells):
+        one_hot = jnp.where((row8 == c) & (lane8 == ids_ref[c]), 1.0, one_hot)
+    hsend[...] = one_hot
     pl.semaphore_wait(barrier, n - 1 + m - 1)
-
-    def one_cell(c, carry):
+    for o in range(1, m):
+        pltpu.make_async_remote_copy(
+            src_ref=hsend,
+            dst_ref=hrecv.at[o],
+            send_sem=late_sem.at[4],
+            recv_sem=late_sem.at[5],
+            device_id=(gene, lax.rem(cell + o, m)),
+            device_id_type=MESH,
+        ).start()
+
+    spans = [slice(i * GROUP, (i + 1) * GROUP) for i in range(groups)]
+
+    def one_cell(c, totals):
         tok_in(c).wait()
         tokens = tok[c]
-        totals = jnp.zeros((latents, LANES), F32)
+        raw = dot(tokens, wk[...])
+        squares = (raw * raw).astype(BF16)
+        values = dot(tokens, wv[...]).astype(BF16)
+        scales = [lax.rsqrt(dot(squares[:, s], mean_head) + EPSILON) for s in spans]
+        keys = [(raw[:, s] * scale).astype(BF16) for s, scale in zip(spans, scales)]
+        weights = [jnp.exp(dot_nt(qb[i], keys[i])) for i in range(groups)]
+        mixes = [dot(weights[i].astype(BF16), values[:, spans[i]]) for i in range(groups)]
         for i in range(groups):
-            cols = slice(i * GROUP, (i + 1) * GROUP)
-            key = dot(tokens, wk[:, cols])
-            key = (key * head_scale(key)).astype(BF16)
-            weights = jnp.exp(dot_nt(qb[i], key))
-            value = dot(tokens, wv[:, cols]).astype(BF16)
-            mixed = dot(weights.astype(BF16), value)
-            total = jnp.sum(weights, axis=1, keepdims=True)
+            mixed = mixes[i]
+            total = jnp.sum(weights[i], axis=1, keepdims=True)
             numerator = mixed[:latents]
             for h in range(per_group):
                 rows = slice(h * latents, (h + 1) * latents)
                 numerator = jnp.where(col_head == h, mixed[rows], numerator)
-                totals = jnp.where(lane == i * per_group + h, total[rows], totals)
+                place = c * heads + i * per_group + h
+                totals = jnp.where(lane == place, total[rows], totals)
             for j in range(n):
-                send[c, j, :, cols] = numerator[j * portion : (j + 1) * portion].astype(BF16)
-        for j in range(n):
-            send[c, j, :, width:] = totals[j * portion : (j + 1) * portion].astype(BF16)
+                send[c, j, :, spans[i]] = numerator[j * portion : (j + 1) * portion].astype(BF16)
         for o in range(1, n):
             peer = lax.rem(gene + o, n)
             pltpu.make_async_remote_copy(
@@ -176,20 +201,28 @@
                 device_id=(peer, cell),
                 device_id_type=MESH,
             ).start()
-        return carry
-
-    lax.fori_loop(0, cells, one_cell, 0)
+        return totals
+
+    totals = lax.fori_loop(0, cells, one_cell, jnp.zeros((latents, LANES), F32))
+    for j in range(n):
+        tsend[j] = totals[j * portion : (j + 1) * portion].astype(BF16)
+    for o in range(1, n):
+        peer = lax.rem(gene + o, n)
+        pltpu.make_async_remote_copy(
+            src_ref=tsend.at[peer],
+            dst_ref=trecv.at[o],
+            send_sem=late_sem.at[6],
+            recv_sem=late_sem.at[7],
+            device_id=(peer, cell),
+            device_id_type=MESH,
+        ).start()
 
     select = iota((cells * portion, latents), 0)
     select = lax.rem(select, portion) + gene * portion == iota((cells * portion, latents), 1)
     own_latents = dot(select.astype(F32).astype(BF16), lat[...])
     mean_latents = jnp.sum(lat[...].astype(F32), axis=0, keepdims=True) * (1.0 / latents)
-    expand = iota((LANES, width), 0) == (iota((LANES, width), 1) >> 6)
+    expand = lax.rem(iota((LANES, width), 0), heads) == (iota((LANES, width), 1) >> 6)
     expand = expand.astype(F32).astype(BF16)
-    one_hot = jnp.zeros((ROWS, LANES), F32)
-    row8, lane8 = iota((ROWS, LANES), 0), iota((ROWS, LANES), 1)
-    for c in range(cells):
-        one_hot = jnp.where((row8 == c) & (lane8 == ids_ref[c]), 1.0, one_hot)
 
     for c in range(cells):
         arrived = pltpu.make_async_remote_copy(
@@ -206,10 +239,25 @@
             total = total + recv[c, o].astype(F32)
         acc[c * portion : (c + 1) * portion, :] = total
         arrived.wait_send()
-    totals = acc[:, width:]
-    is_head = iota(totals.shape, 1) < heads
-    inverse = jnp.where(is_head, 1.0 / jnp.where(is_head, totals, 1.0), 0.0)
-    attended = (acc[:, :width] * dot_split(inverse, expand)).astype(BF16)
+    arrived = pltpu.make_async_remote_copy(
+        src_ref=trecv.at[pl.ds(1, n - 1)],
+        dst_ref=trecv.at[pl.ds(1, n - 1)],
+        send_sem=late_sem.at[6],
+        recv_sem=late_sem.at[7],
+        device_id=(gene, cell),
+        device_id_type=MESH,
+    )
+    arrived.wait_recv()
+    totals = tsend[gene].astype(F32)
+    for o in range(1, n):
+        totals = totals + trecv[o].astype(F32)
+    arrived.wait_send()
+    place = iota((portion, LANES), 1)
+    inverse = 1.0 / jnp.where(place < cells * heads, totals, 1.0)
+    for c in range(cells):
+        own = (place >= c * heads) & (place < (c + 1) * heads)
+        inv[c * portion : (c + 1) * portion, :] = jnp.where(own, inverse, 0.0)
+    attended = (acc[...] * dot_split(inv[...], expand)).astype(BF16)
     wide = attended.astype(F32)
     for c in range(cells):
         row = jnp.sum(wide[c * portion : (c + 1) * portion], axis=0, keepdims=True)
@@ -246,12 +294,12 @@
     for o in range(1, n):
         summed = summed + precv[o].astype(F32)
     arrived.wait_send()
-    summed = jnp.concatenate([summed, pltpu.roll(summed, ROWS - cells, 0)], axis=1)
-    pooled = mean_latents + dot_split(summed * (1.0 / latents), wo[...])
+    pooled = mean_latents + dot_split(side_by_side(summed) * (1.0 / latents), wo[...])
     scale = lax.rsqrt(jnp.mean(pooled * pooled, axis=1, keepdims=True) + EPSILON)
     own_input = (pooled * scale).astype(BF16)
-    ssend[:, :width] = own_input.astype(F32)
-    ssend[:, width:] = one_hot
+    own_wide = own_input.astype(F32)
+    second = pltpu.roll(own_wide[:, half:], cells, 0)
+    ssend[...] = jnp.where(iota((ROWS, half), 0) < cells, own_wide[:, :half], second).astype(BF16)
     for o in range(1, m):
         pltpu.make_async_remote_copy(
             src_ref=ssend,
@@ -285,9 +333,20 @@
         device_id_type=MESH,
     )
     arrived.wait_recv()
-    every = jnp.concatenate([ssend[...]] + [srecv[o] for o in range(1, m)], axis=0).astype(BF16)
+    parts = [own_wide] + [side_by_side(srecv[o].astype(F32)) for o in range(1, m)]
+    every_input = jnp.concatenate(parts, axis=0).astype(BF16)
     arrived.wait_send()
-    every_input, key_sets = every[:, :width], every[:, width:]
+    arrived = pltpu.make_async_remote_copy(
+        src_ref=hrecv.at[pl.ds(1, m - 1)],
+        dst_ref=hrecv.at[pl.ds(1, m - 1)],
+        send_sem=late_sem.at[4],
+        recv_sem=late_sem.at[5],
+        device_id=(gene, cell),
+        device_id_type=MESH,
+    )
+    arrived.wait_recv()
+    key_sets = jnp.concatenate([one_hot] + [hrecv[o] for o in range(1, m)], axis=0).astype(BF16)
+    arrived.wait_send()
     keys_values = dot(every_input, wqkv[:, width:])
     keys = head_rows(keys_values[:, :width]).astype(BF16)
     values = keys_values[:, width:].astype(BF16)
@@ -311,7 +370,6 @@
     portion = rows // n
     hbm = pl.BlockSpec(memory_space=pltpu.HBM)
     vmem = pl.BlockSpec(memory_space=pltpu.VMEM)
-    wide = width + LANES
     return tuple(
         pl.pallas_call(
             functools.partial(kernel, n, m),
@@ -330,21 +388,26 @@
                 pltpu.VMEM(w_set_qkv.shape, BF16),
                 pltpu.VMEM(w_set_out.shape, BF16),
                 pltpu.VMEM((width // GROUP, GROUP, GROUP), BF16),
-                pltpu.VMEM((cells, n, portion, wide), BF16),
-                pltpu.VMEM((cells, n, portion, wide), BF16),
-                pltpu.VMEM((cells * portion, wide), F32),
+                pltpu.VMEM((cells, n, portion, width), BF16),
+                pltpu.VMEM((cells, n, portion, width), BF16),
+                pltpu.VMEM((cells * portion, width), F32),
                 pltpu.VMEM((ROWS, width // 2), F32),
                 pltpu.VMEM((ROWS, width // 2), BF16),
                 pltpu.VMEM((n, ROWS, width // 2), BF16),
-                pltpu.VMEM((ROWS, wide), F32),
-                pltpu.VMEM((m, ROWS, wide), F32),
+                pltpu.VMEM((ROWS, width // 2), BF16),
+                pltpu.VMEM((m, ROWS, width // 2), BF16),
+                pltpu.VMEM((n, portion, LANES), BF16),
+                pltpu.VMEM((n, portion, LANES), BF16),
+                pltpu.VMEM((ROWS, LANES), F32),
+                pltpu.VMEM((m, ROWS, LANES), F32),
+                pltpu.VMEM((cells * portion, LANES), F32),
                 pltpu.SMEM(head_temp.shape, F32),
                 pltpu.SMEM(set_ids.shape, jnp.int32),
                 pltpu.SemaphoreType.DMA((8,)),
                 pltpu.SemaphoreType.DMA((cells,)),
                 pltpu.SemaphoreType.DMA((cells,)),
                 pltpu.SemaphoreType.DMA((cells,)),
-                pltpu.SemaphoreType.DMA((4,)),
+                pltpu.SemaphoreType.DMA((8,)),
             ],
             compiler_params=pltpu.CompilerParams(
                 collective_id=0, has_side_effects=True, vmem_limit_bytes=VMEM_BYTES

time: 39 us -> 32.7 us (0.84)
  Pallas kernels: 35.5 us -> 29.2 us
    pallas_call x1, Pallas kernels: 35.5 us -> 29.2 us  [on_device(): pl.pallas_call(functools.partial(kernel, n, m), out_shape=(jax.ShapeDtype...]
where the time goes in v3:
time: 32.7 us; the launch traced here: 32.5 us
  Pallas kernels  29.2 us (89%)
  local copies, waits for them, and re-layouts  2.71 us (8%)
  between operations  0.64 us (2%)
    pallas_call x1, Pallas kernels, on_device(): pl.pallas_call(functools.partial(kernel, n, m), out_shape=(jax.ShapeDtype...  29.2 us
    unnamed x2, local copies, waits for them, and re-layouts  2.71 us

profile of v3, /device:TPU:0, one launch (start us, length us, event | category | flops | bytes accessed | tf_op | source)
XLA Modules:
  0.0 32.5 jit_solution(2512854888519339487)
XLA Ops:
  0.6 29.2 %latent_cross_attention.1 = (bf16[4,8,768]{2,1,0:T(8,128)(2,1)}, bf16[4,768]{1,0:T(4,128)(2,1)}) custom-call(bf16[4,512,768]{2,1,0:T(8,128)(2,1)} %tok_hbm.1, bf16[64,768]{1,0:T(8,128)(2,1)} %lat_hbm.1, f32[12]{0:T(128)} %temp_hbm.1, bf16[768,768]{1,0:T(8,128)(2,1)} %wk_hbm.1, bf16[768,768]{1,0:T(8,128)(2,1)} %wv_hbm.1, bf16[768,768]{1,0:T(8,128)(2,1)} %wo_hbm.1, ...), custom_call_target="tpu_custom_call" | custom-call | tf_op jit(solution)/shard_map/latent_cross_attention/pallas_call | solution.py:374
  29.8 1.4 %copy.13 = bf16[4,8,768]{2,1,0:T(8,128)(2,1)} copy(bf16[4,8,768]{2,1,0:T(8,128)(2,1)} %get-tuple-element.4) | data formatting | bytes 98304
  31.2 1.3 %copy.14 = bf16[4,768]{1,0:T(4,128)(2,1)} copy(bf16[4,768]{1,0:T(4,128)(2,1)} %get-tuple-element.5) | data formatting | bytes 12288

commit v4 on v3

--- a/solution.py
+++ b/solution.py
@@ -14,7 +14,7 @@
 HEAD = 64
 LANES = 128
 GROUP = 256
-VMEM_BYTES = 63 * 1024 * 1024
+VMEM_BYTES = 58 * 1024 * 1024
 ROWS = 8
 
 
@@ -374,8 +374,8 @@
         pl.pallas_call(
             functools.partial(kernel, n, m),
             out_shape=(
-                jax.ShapeDtypeStruct((cells, portion, width), BF16),
-                jax.ShapeDtypeStruct((cells, width), BF16),
+                pltpu.VMEM((cells, portion, width), BF16),
+                pltpu.VMEM((cells, width), BF16),
             ),
             in_specs=[hbm] * 9,
             out_specs=(vmem, vmem),

time: 32.7 us -> 30.6 us (0.936)
  local copies, waits for them, and re-layouts: 2.71 us -> 1.22 us
  Pallas kernels: 29.2 us -> 28.6 us
    unnamed x2, local copies, waits for them, and re-layouts: 2.71 us -> 1.22 us
    pallas_call x1, Pallas kernels: 29.2 us -> 28.6 us  [on_device(): pl.pallas_call(functools.partial(kernel, n, m), out_shape=(pltpu.VMEM((ce...]
where the time goes in v4:
time: 30.6 us; the launch traced here: 30.4 us
  Pallas kernels  28.6 us (93%)
  local copies, waits for them, and re-layouts  1.22 us (4%)
  between operations  0.64 us (2%)
    pallas_call x1, Pallas kernels, on_device(): pl.pallas_call(functools.partial(kernel, n, m), out_shape=(pltpu.VMEM((ce...  28.6 us
    unnamed x2, local copies, waits for them, and re-layouts  1.22 us

profile of v4, /device:TPU:0, one launch (start us, length us, event | category | flops | bytes accessed | tf_op | source)
XLA Modules:
  0.0 30.4 jit_solution(7888481754654163524)
XLA Ops:
  0.6 28.6 %latent_cross_attention.1 = (bf16[4,8,768]{2,1,0:T(8,128)(2,1)S(1)}, bf16[4,768]{1,0:T(4,128)(2,1)S(1)}) custom-call(bf16[4,512,768]{2,1,0:T(8,128)(2,1)} %tok_hbm.1, bf16[64,768]{1,0:T(8,128)(2,1)} %lat_hbm.1, f32[12]{0:T(128)} %temp_hbm.1, bf16[768,768]{1,0:T(8,128)(2,1)} %wk_hbm.1, bf16[768,768]{1,0:T(8,128)(2,1)} %wv_hbm.1, bf16[768,768]{1,0:T(8,128)(2,1)} %wo_hbm.1, ...), custom_call_target="tpu_custom_call" | custom-call | tf_op jit(solution)/shard_map/latent_cross_attention/pallas_call | solution.py:374
  29.2 0.6 %copy.13 = bf16[4,8,768]{2,1,0:T(8,128)(2,1)} copy(bf16[4,8,768]{2,1,0:T(8,128)(2,1)S(1)} %get-tuple-element.2) | data formatting | bytes 98304
  29.8 0.6 %copy.14 = bf16[4,768]{1,0:T(4,128)(2,1)} copy(bf16[4,768]{1,0:T(4,128)(2,1)S(1)} %get-tuple-element.3) | data formatting | bytes 12288
